TPU v7x, 256 devices: a whole 4x4x8 slice. The times are simulated.
256 devices in a mesh: img: 64 (over y, z_lo, x, core), slab: 4 (over z_hi).
Axes of the slice: x: 4, y: 4, z: 8 (z_hi: 4, z_lo: 2; z = z_hi * 2 + z_lo), core: 2. Of those that a mesh axis runs over, the one named last changes fastest.
Arguments:
- images: bfloat16 [4096, 32768], P('img'), may hold values from -6 to 6
- references: bfloat16 [2, 128, 32768], P(None, 'slab'), may hold values from -6 to 6
- orientations: int32 [4096, 2, 64], P('img'), may hold values from 0 to 127
- ctf_table: float32 [4096, 64], P('img'), may hold values from -1 to 1
- inv_noise: float32 [4096], P('img'), may hold values from 0.002 to 0.02
- class_weight: float32 [2], replicated, may hold values from 0.2 to 5
Outputs:
- updated_volume: float32 [2, 128, 32768], P(None, 'slab', 'img')
All inputs are finite; a program needn't handle non-finite values.
Results may differ from a plain program's by a relative error of at most 0.0065.
Values sent between devices are 32-bit elements; how exact they have to be, the bound alone decides.
A program may use at most 192 MiB of HBM per device.

v0:
```python
import jax
import jax.numpy as jnp
from jax import lax
from jax.sharding import PartitionSpec as P

BOX = 128
SHELLS = 64


def shell_index():
    position = jnp.arange(BOX * BOX, dtype=jnp.int32)
    column = position % BOX - BOX // 2
    row_place = position // BOX - BOX // 2
    radius_sq = column * column + row_place * row_place
    levels = jnp.arange(1, SHELLS, dtype=jnp.int32)
    inside = (2 * levels[None, :] * levels[None, :] <= radius_sq[:, None]).astype(jnp.int32)
    return jnp.sum(inside, axis=1)


def contract_first(left, right):
    return lax.dot_general(
        left, right, (((0,), (0,)), ((), ())), preferred_element_type=jnp.float32
    )


def contract_last(left, right):
    return lax.dot_general(
        left, right, (((1,), (1,)), ((), ())), preferred_element_type=jnp.float32
    )


def shards(images, references, orientations, ctf_table, inv_noise, class_weight):
    batch = images.shape[0]
    classes, local_planes, width = references.shape
    pixels = width // 2
    levels = jnp.arange(SHELLS, dtype=jnp.int32)
    selector = (shell_index()[None, :] == levels[:, None]).astype(jnp.float32)
    ctf_pixel = jnp.dot(
        ctf_table, selector, precision=lax.Precision.HIGHEST, preferred_element_type=jnp.float32
    )
    weighted = (images.astype(jnp.float32) * jnp.repeat(ctf_pixel, 2, axis=1)).astype(jnp.bfloat16)
    ctf_square = (ctf_pixel * ctf_pixel).astype(jnp.bfloat16)
    planes = references.reshape(classes * local_planes, width)
    spread = references.astype(jnp.float32).reshape(classes * local_planes, pixels, 2)
    power = jnp.sum(spread * spread, axis=2).astype(jnp.bfloat16)
    intersection = contract_last(weighted, planes)
    energy = contract_last(ctf_square, power)
    local_table = (2.0 * intersection - energy).reshape(batch, classes, local_planes)
    offset = lax.axis_index("slab") * local_planes
    relative = orientations - offset
    inside = (relative >= 0) & (relative < local_planes)
    prior = jnp.log(class_weight)[None, :, None]
    table = lax.all_gather(local_table, "slab", axis=2, tiled=True)
    picked = jnp.take_along_axis(table, orientations, axis=2)
    scores = prior + inv_noise[:, None, None] * picked
    peak = jnp.max(scores, axis=(1, 2), keepdims=True)
    expo = jnp.exp(scores - peak)
    resp = expo / jnp.sum(expo, axis=(1, 2), keepdims=True)
    local_resp = jnp.where(inside, resp, 0.0)
    plane_ids = jnp.arange(local_planes, dtype=jnp.int32)
    hits = (relative[:, :, :, None] == plane_ids[None, None, None, :]).astype(jnp.float32)
    per_plane = jnp.einsum("bkl,bklp->bkp", local_resp, hits).astype(jnp.bfloat16)
    flat_plane = per_plane.reshape(batch, classes * local_planes)
    planes_here = classes * local_planes
    share = width // lax.axis_size("img")
    square_pairs = jnp.repeat(ctf_square, 2, axis=1)
    summed = lax.psum_scatter(
        jnp.concatenate(
            [contract_first(weighted, flat_plane), contract_first(square_pairs, flat_plane)], axis=1
        ),
        "img",
        scatter_dimension=0,
        tiled=True,
    )
    numerator = summed[:, :planes_here]
    weight_sum = summed[:, planes_here:]
    updated = numerator / (weight_sum + 1.0)
    return jnp.transpose(updated).reshape(classes, local_planes, share)


def solution(mesh):
    return jax.shard_map(
        shards,
        mesh=mesh,
        in_specs=(
            P("img", None),
            P(None, "slab", None),
            P("img", None, None),
            P("img", None),
            P("img"),
            P(),
        ),
        out_specs=P(None, "slab", "img"),
        check_vma=False,
    )
```

profile of v0, /device:TPU:2, one launch (start us, length us, event | category | flops | bytes accessed | tf_op | source)
XLA Modules:
  0.0 651.1 jit_solution(16767141017079133494)
XLA Ops:
  6.6 0.6 convert_reduce_fusion
  7.2 0.1 copy-done
  7.3 3.9 multiply_convert_fusion.1
  11.2 6.9 %copy.33 = f32[64,16384]{0,1:T(8,128)} copy(f32[64,16384]{1,0:T(8,128)} %get-tuple-element.10) | data formatting | bytes 8388608 | tf_op jit(solution)/shard_map/dot_general | solution.py:38
  18.1 8.4 %copy.32 = bf16[64,32768]{0,1:T(8,128)(2,1)} copy(bf16[64,32768]{1,0:T(8,128)(2,1)} %param.6) | data formatting | bytes 8388608 | tf_op args[0]
  26.5 6.0 convert_multiply_fusion
  32.4 37.3 %copy.34 = f32[2,32,32768]{1,0,2:T(2,128)} copy(f32[2,32,32768]{2,1,0:T(8,128)} %convert_multiply_fusion) | data formatting | bytes 16777216 | tf_op jit(solution)/shard_map/mul | solution.py:45
  69.8 37.1 %mul.74 = f32[64,16384,2]{0,2,1:T(2,128)} reshape(f32[2,32,32768]{1,0,2:T(2,128)} %copy.34) | data formatting | bytes 16777216 | tf_op jit(solution)/shard_map/mul | solution.py:45
  106.9 3.2 copy.37
  110.1 73.2 %reduce_sum.28 = bf16[64,16384]{0,1:T(8,128)(2,1)} reduce(f32[64,16384,2]{0,2,1:T(2,128)} %mul.74, f32[]{:T(128)} %constant.64.clone.1), dimensions={2}, to_apply=%region_1.2 | reduce | flops 1048576 | bytes 10485764 | tf_op jit(solution)/shard_map/reduce_sum | solution.py:45
  183.2 9.6 %broadcast_in_dim.11 = f32[64,16384,2]{0,2,1:T(2,128)} broadcast(f32[64,16384]{0,1:T(8,128)} %copy.33), dimensions={0,1} | broadcast | bytes 12582912 | tf_op jit(solution)/shard_map/broadcast_in_dim | solution.py:41
  192.8 0.3 copy-done.3
  193.1 10.8 %convolution_multiply_fusion = f32[64,64]{1,0:T(8,128)S(1)} fusion(bf16[64,32768]{1,0:T(8,128)(2,1)S(1)} %bitcast.33, f32[64,32768]{0,1:T(8,128)} %bitcast.30, bf16[64,32768]{0,1:T(8,128)(2,1)} %copy.32), kind=kOutput, calls=%fused_computation.14 | convolution fusion | flops 274731008 | bytes 16793600 | tf_op jit(solution)/shard_map/dot_general | solution.py:27
  204.0 3.1 fusion.4
  207.1 0.1 copy.35
  207.2 17.4 %all_gather.3 = f32[64,2,128]{0,1,2:T(2,128)S(1)} all-gather(f32[64,2,32]{0,1,2:T(2,128)S(1)} %copy.36), channel_id=1, replica_groups=mesh['img'=64,'slab'=4] {'slab'}, dimensions={2}, use_global_device_ids=true | all-gather | bytes 81920 | tf_op jit(solution)/shard_map/all_gather | solution.py:53
  224.6 0.1 bitcast_or_fusion
  224.7 0.1 reshape.75
  224.8 74.9 %gather_fusion = f32[8192]{0:T(1024)S(1)} fusion(f32[64,2,128]{0,1,2:T(2,128)S(1)} %all_gather.3, s32[8192]{0:T(1024)S(1)} %reshape.75), kind=kCustom, calls=%fused_computation | custom fusion | bytes 163840 | tf_op jit(solution)/shard_map/jit(take_along_axis)/gather | solution.py:54
  299.7 0.1 reshape.78
  299.8 0.9 fusion.25
  300.8 1.0 fusion.23
  301.7 0.2 and_select_fusion.1
  302.0 0.7 fusion.3
  302.6 0.1 copy.39
  302.7 11.3 %fusion.24 = f32[32768,64]{0,1:T(8,128)S(1)} fusion(bf16[64,64]{0,1:T(8,128)(2,1)S(1)} %bitcast.34, f32[64,32768]{0,1:T(8,128)} %bitcast.31, bf16[64,32768]{0,1:T(8,128)(2,1)} %copy.32), kind=kOutput, calls=%fused_computation.45 | convolution fusion | flops 274726912 | bytes 20979712 | tf_op jit(solution)/shard_map/dot_general | solution.py:21
  314.1 5.6 broadcast_in_dim.15
  319.6 6.4 fusion.27
  326.0 6.1 pad_maximum_fusion
  332.1 0.0 reduce-scatter.2.cloned.1.call-update
  332.1 310.4 %reduce-scatter.2.cloned.1.call-done = f32[512,128]{0,1:T(8,128)} async-done(((f32[32768,128]{0,1:T(8,128)}), f32[512,128]{0,1:T(8,128)}) %reduce-scatter.2.cloned.1.call-update) | async-done | bytes 262160 | tf_op jit(solution)/shard_map/reduce_scatter | solution.py:67
  642.6 1.6 fusion.8
  (17 shorter events, 0.1 us)
Async XLA Ops:
  6.5 0.8 copy-start
  6.5 636.0 %reduce-scatter.2.cloned.1.call-start = ((), (), s32[]{:S(2)}) async-start(), calls=%async_computation.1 | async-start | bytes 17039360 | tf_op jit(solution)/shard_map/reduce_scatter | solution.py:67
  183.2 9.9 %copy-start.3 = (bf16[2,32,32768]{2,1,0:T(8,128)(2,1)S(1)}, bf16[2,32,32768]{2,1,0:T(8,128)(2,1)}, u32[]{:S(2)}) copy-start(bf16[2,32,32768]{2,1,0:T(8,128)(2,1)} %param.7) | copy-start | bytes 12582916
  204.0 20.6 %copy-start.4 = (s32[64,2,64]{2,1,0:T(2,128)S(1)}, s32[64,2,64]{2,1,0:T(2,128)}, u32[]{:S(2)}) copy-start(s32[64,2,64]{2,1,0:T(2,128)} %param.8) | copy-start | bytes 98308
  224.8 75.0 %copy-start.6 = (f32[2]{0:T(128)S(1)}, f32[2]{0:T(128)}, u32[]{:S(2)}) copy-start(f32[2]{0:T(128)} %param.11) | copy-start | bytes 28
  224.8 75.0 %copy-start.5 = (f32[64]{0:T(128)S(1)}, f32[64]{0:T(128)}, u32[]{:S(2)}) copy-start(f32[64]{0:T(128)} %param.10) | copy-start | bytes 772
  302.7 11.3 %copy-start.2 = (bf16[64,16384]{0,1:T(8,128)(2,1)S(1)}, bf16[64,16384]{0,1:T(8,128)(2,1)}, u32[]{:S(2)}) copy-start(bf16[64,16384]{0,1:T(8,128)(2,1)} %copy.37) | copy-start | bytes 6291460
  332.1 312.1 %copy-start.1 = (f32[64,64]{1,0:T(8,128)S(1)}, f32[64,64]{1,0:T(8,128)}, u32[]{:S(2)}) copy-start(f32[64,64]{1,0:T(8,128)} %param.9) | copy-start | bytes 49156
Sparse Core Ops, SparseCore 0:
  332.3 310.2 reduce-scatter.1
where the time goes:
time: 658 us; the launch traced here: 651 us
  waiting for transfers between devices  310 us (47%)
  local copies, waits for them, and re-layouts  184 us (28%)
  other arithmetic  89.7 us (14%)
  matrix products  36.2 us (6%)
  blocking collectives  17.4 us (3%)
  between operations  13.5 us (2%)
    reduce_scatter x1, waiting for transfers between devices, shards(): lax.psum_scatter(jnp.concatenate([contract_first(weighted, flat_plane), c...  310 us
    gather x3, local copies, waits for them, and re-layouts, shards(): picked = jnp.take_along_axis(table, orientations, axis=2)  75.1 us
    mul x2, local copies, waits for them, and re-layouts, shards(): power = jnp.sum(spread * spread, axis=2).astype(jnp.bfloat16)  74.5 us
    reduce_sum x1, other arithmetic, shards(): power = jnp.sum(spread * spread, axis=2).astype(jnp.bfloat16)  73.2 us
    dot_general x2, matrix products, contract_first(): lax.dot_general(left, right, (((0,), (0,)), ((), ())), preferred_element_...  17.7 us
    all_gather x1, blocking collectives, shards(): table = lax.all_gather(local_table, 'slab', axis=2, tiled=True)  17.4 us
    dot_general x2, matrix products, contract_last(): lax.dot_general(left, right, (((1,), (1,)), ((), ())), preferred_element_...  13.9 us
  transfers between devices with their start and end apart: 1, of which 1 were waited for; matrix products, arithmetic and copies ran while one was open for 0% of the time, Pallas kernels for 0%

commit v1 on v0

v1 whole, which is shorter than its diff:
```python
import functools

import jax
import jax.numpy as jnp
from jax import lax
from jax.experimental import pallas as pl
from jax.experimental.pallas import tpu as pltpu
from jax.sharding import PartitionSpec as P

BOX = 128
SHELLS = 64
KP = 64
IMG = 64
WIDTH = 32768
BLOCK = 512
CHUNK = 4096
STEPS = WIDTH // CHUNK
PER_STEP = CHUNK // (2 * BLOCK)
ROWS = 8
UNITS = KP // 2 // ROWS
HALF = 256
LOWEST = -3.0e38
MESH = pl.DeviceIdType.MESH
F32 = jnp.float32
BF16 = jnp.bfloat16


def lanes(table, index):
    return jnp.take_along_axis(table, index, axis=1, mode="promise_in_bounds")


def flat(core, x, z, y):
    return ((y * 2 + z) * 4 + x) * 2 + core


def kernel(
    img_hbm, ref_hbm, orient_ref, ctf_ref, noise_ref, prior_ref, out_ref,
    img_v, ref_v, wall, w_send, w_recv, ctf_other, stat_send, stat_own, stat_other, pair_recv,
    part_a, part_b, part_c, fwd_a, dir_a, sum_a, fwd_b, dir_b, sum_b, z_recv,
    tot, tot_recv, counts,
    img_sem, ref_sem, w_ssem, w_rsem, s_ssem, s_rsem, a_ssem, a_rsem, b_ssem, b_rsem, t_ssem, t_rsem,
):
    mine = lax.axis_index("img")
    slab = lax.axis_index("slab")
    core, x = mine % 2, (mine // 2) % 4
    z, y = (mine // 8) % 2, mine // 16

    def at_x(d):
        return (flat(core, (x + d) % 4, z, y), slab)

    def at_y(d):
        return (flat(core, x, z, (y + d) % 4), slab)

    at_z = (flat(core, x, 1 - z, y), slab)
    sibling = (flat(1 - core, x, z, y), slab)

    loads = []
    for g in range(STEPS):
        span = pl.ds(g * CHUNK, CHUNK)
        loads.append(pltpu.make_async_copy(img_hbm.at[:, span], img_v.at[g], img_sem.at[g]))
        loads.append(pltpu.make_async_copy(ref_hbm.at[:, span], ref_v.at[g], ref_sem.at[g]))
    for load in loads:
        load.start()

    peers = [sibling, at_z]
    peers += [at_x(d) for d in (1, 2, 3)] + [at_y(d) for d in (1, 2, 3)]
    for d in (1, 2, 3):
        peers.append((mine, (slab + d) % 4))
        peers.append((flat(1 - core, x, z, y), (slab + d) % 4))
    barrier = pltpu.get_barrier_semaphore()
    for peer in peers:
        pl.semaphore_signal(barrier, inc=1, device_id=peer, device_id_type=MESH)

    own = jnp.concatenate([orient_ref[:, 0, :], orient_ref[:, 1, :]], axis=1).astype(F32)
    own = jnp.transpose(own) - (slab * 32).astype(F32)
    for k in range(2):
        listed = own[k * 64:(k + 1) * 64]
        for p in range(32):
            hit = jnp.where(listed == float(p), 1.0, 0.0)
            counts[k * 32 + p:k * 32 + p + 1, :] = jnp.sum(hit, axis=0, keepdims=True)

    pl.semaphore_wait(barrier, len(peers))

    used = {"a": 0, "b": 0, "s": 0, "t": 0}
    sems = {"a": (a_ssem, a_rsem), "b": (b_ssem, b_rsem), "s": (s_ssem, s_rsem), "t": (t_ssem, t_rsem)}
    sent = []

    def send(kind, src, dst, peer):
        n = used[kind]
        used[kind] = n + 1
        copy = pltpu.make_async_remote_copy(
            src_ref=src, dst_ref=dst, send_sem=sems[kind][0].at[n], recv_sem=sems[kind][1].at[n],
            device_id=peer, device_id_type=MESH,
        )
        copy.start()
        sent.append(copy)
        return copy

    ctf_copy = send("s", ctf_ref, ctf_other, sibling)

    table = jnp.concatenate([ctf_ref[...], jnp.zeros((IMG, 64), F32)], axis=1)
    lane = lax.broadcasted_iota(jnp.int32, (8, 128), 1)
    near = (lane // 2 - 64).astype(F32)
    far = (lane // 2).astype(F32)
    squares = (0.5 * near * near + 0.25, 0.5 * far * far + 0.25)
    even = lax.broadcasted_iota(jnp.int32, (KP, 128), 1) % 2 == 0

    def shells(column, b):
        row = (column + b * 128) // 256 - 64
        radius = squares[b % 2] + 0.5 * (row * row).astype(F32)
        return jnp.minimum(jnp.sqrt(radius), 63.0).astype(jnp.int32)

    def w_copy(g):
        span = pl.ds(g * PER_STEP, PER_STEP)
        return pltpu.make_async_remote_copy(
            src_ref=w_send.at[span], dst_ref=w_recv.at[span], send_sem=w_ssem.at[g], recv_sem=w_rsem.at[g],
            device_id=sibling, device_id_type=MESH,
        )

    def score(g, carry):
        fit, energy = carry
        pltpu.make_async_copy(img_hbm.at[:, pl.ds(0, CHUNK)], img_v.at[g], img_sem.at[g]).wait()
        pltpu.make_async_copy(ref_hbm.at[:, pl.ds(0, CHUNK)], ref_v.at[g], ref_sem.at[g]).wait()
        for other in (True, False):
            part = 1 - core if other else core
            for n in range(PER_STEP):
                inner = pl.multiple_of(n * 2 * BLOCK + part * BLOCK, BLOCK)
                pixels = img_v[g, :, pl.ds(inner, BLOCK)]
                entries = ref_v[g, :, pl.ds(inner, BLOCK)]
                ws, cs, ps = [], [], []
                for b in range(BLOCK // 128):
                    cut = slice(b * 128, (b + 1) * 128)
                    index = jnp.concatenate([shells(g * CHUNK + inner, b)] * 8, axis=0)
                    ctf = lanes(table, index)
                    ws.append((pixels[:, cut].astype(F32) * ctf).astype(BF16))
                    cs.append((ctf * ctf).astype(BF16))
                    wide = entries[:, cut].astype(F32)
                    wide = wide * wide
                    both = wide + pltpu.roll(wide, 127, 1)
                    ps.append(jnp.where(even, both, 0.0).astype(BF16))
                w = jnp.concatenate(ws, axis=1)
                c = jnp.concatenate(cs, axis=1)
                p = jnp.concatenate(ps, axis=1)
                fit = fit + lax.dot_general(entries, w, (((1,), (1,)), ((), ())), preferred_element_type=F32)
                energy = energy + lax.dot_general(p, c, (((1,), (1,)), ((), ())), preferred_element_type=F32)
                t = g * PER_STEP + n
                if other:
                    w_send[t] = w.astype(F32)
                else:
                    wall[t, 0:IMG, :] = w
            if other:
                w_copy(g).start()
        return fit, energy

    zero = jnp.zeros((KP, IMG), F32)
    fit, energy = lax.fori_loop(0, STEPS, score, (zero, zero))

    upper = lax.broadcasted_iota(jnp.int32, (KP, IMG), 0) < 32
    prior = jnp.log(jnp.where(upper, prior_ref[0], prior_ref[1]))
    value = prior + noise_ref[...] * (2.0 * fit - energy)
    count = counts[...]
    listed = count > 0.0
    peak = jnp.max(jnp.where(listed, value, LOWEST), axis=0, keepdims=True)
    weight = jnp.where(listed, count * jnp.exp(value - peak), 0.0)
    mass = jnp.sum(weight, axis=0, keepdims=True)
    stat_send[0:KP, 0:IMG] = weight
    stat_send[KP:KP + 1, 0:IMG] = peak
    stat_send[KP + 1:KP + 2, 0:IMG] = mass
    stats = stat_send.at[pl.ds(KP, 8), :]
    waits = []
    for d in (1, 2, 3):
        waits.append(send("s", stats, stat_own.at[d - 1], (mine, (slab + d) % 4)))
        waits.append(send("s", stats, stat_other.at[d - 1], (flat(1 - core, x, z, y), (slab + d) % 4)))
    waits.append(send("s", stat_send, pair_recv, sibling))

    def widen(g, carry):
        w_copy(g).wait()
        for n in range(PER_STEP):
            t = g * PER_STEP + n
            wall[t, IMG:2 * IMG, :] = w_recv[t].astype(BF16)
        return carry

    lax.fori_loop(0, STEPS, widen, 0)
    ctf_copy.wait_recv()
    squared = jnp.concatenate([ctf_ref[...], ctf_other[...]], axis=0)
    squared = (squared * squared).astype(BF16)
    for copy in waits:
        copy.wait_recv()

    def share(first, second, rest):
        top = first
        for d in range(3):
            top = jnp.maximum(top, rest[d, 0:1, 0:IMG])
        total = second * jnp.exp(first - top)
        for d in range(3):
            total = total + rest[d, 1:2, 0:IMG] * jnp.exp(rest[d, 0:1, 0:IMG] - top)
        return jnp.exp(first - top) / total

    here = weight * share(peak, mass, stat_own)
    there = pair_recv[0:KP, 0:IMG] * share(pair_recv[KP:KP + 1, 0:IMG], pair_recv[KP + 1:KP + 2, 0:IMG], stat_other)
    planes = jnp.concatenate([here, there], axis=1).astype(BF16)

    shell_sum = jnp.dot(planes, squared, preferred_element_type=F32)
    tot[0] = jnp.concatenate([shell_sum[0:32], shell_sum[32:64]], axis=1)
    tot_x = [send("t", tot.at[0], tot_recv.at[d - 1], at_x(d)) for d in (1, 2, 3)]

    def block(dx, dy, dz):
        t = (((y + dy) % 4) * 2 + (z + dz) % 2) * 4 + (x + dx) % 4
        got = jnp.dot(planes, wall[t], preferred_element_type=F32)
        for h in range(2):
            cut = slice(h * HALF, (h + 1) * HALF)
            for u in range(UNITS):
                part_a[0, u, h, dx, dy, dz] = got[u * ROWS:(u + 1) * ROWS, cut]
                low = (UNITS + u) * ROWS
                part_a[1, u, h, dy, dx, dz] = got[low:low + ROWS, cut]

    at = (at_x, at_y)
    units = [(o, u) for u in range(UNITS) for o in range(2)]
    f_a, g_a, h_a, f_b, g_b, h_b, z_c = {}, {}, {}, {}, {}, {}, {}

    def first_a(o, u):
        f_a[o, u] = [
            send("a", part_a.at[o, u, 0, 2], fwd_a.at[o, u, 0], at[o](1)),
            send("a", part_a.at[o, u, 1, 2], fwd_a.at[o, u, 1], at[o](3)),
        ]

    def direct_a(o, u):
        g_a[o, u] = [
            send("a", part_a.at[o, u, 1, 1], dir_a.at[o, u, 1], at[o](1)),
            send("a", part_a.at[o, u, 0, 3], dir_a.at[o, u, 0], at[o](3)),
        ]

    def second_a(o, u):
        h_a[o, u] = []
        for h, d in ((0, 1), (1, 3)):
            f_a[o, u][h].wait_recv()
            part_a[o, u, h, d] = part_a[o, u, h, d] + fwd_a[o, u, h]
            h_a[o, u].append(send("a", part_a.at[o, u, h, d], sum_a.at[o, u, h], at[o](d)))

    def last_a(o, u):
        for h in range(2):
            g_a[o, u][1 - h].wait_recv()
            h_a[o, u][h].wait_recv()
            part_b[o, u, h] = part_a[o, u, h, 0] + dir_a[o, u, h] + sum_a[o, u, h]

    def first_b(o, u):
        to = at[1 - o]
        f_b[o, u] = [
            send("b", part_b.at[o, u, 0, 2], fwd_b.at[o, u, 0], to(1)),
            send("b", part_b.at[o, u, 1, 2], fwd_b.at[o, u, 1], to(3)),
        ]
        g_b[o, u] = [
            send("b", part_b.at[o, u, 1, 1], dir_b.at[o, u, 1], to(1)),
            send("b", part_b.at[o, u, 0, 3], dir_b.at[o, u, 0], to(3)),
        ]

    def second_b(o, u):
        to = at[1 - o]
        h_b[o, u] = []
        for h, d in ((0, 1), (1, 3)):
            f_b[o, u][h].wait_recv()
            part_b[o, u, h, d] = part_b[o, u, h, d] + fwd_b[o, u, h]
            h_b[o, u].append(send("b", part_b.at[o, u, h, d], sum_b.at[o, u, h], to(d)))

    def last_b(o, u):
        for h in range(2):
            g_b[o, u][1 - h].wait_recv()
            h_b[o, u][h].wait_recv()
            done = part_b[o, u, h, 0] + dir_b[o, u, h] + sum_b[o, u, h]
            for dz in range(2):
                part_c[o, u, dz, h] = done[dz]
        z_c[o, u] = send("b", part_c.at[o, u, 1], z_recv.at[o, u], at_z)

    for dy in (2, 1, 3, 0):
        for dz in range(2):
            block(2, dy, dz)
    for u in range(UNITS):
        first_a(0, u)
    for dx in (1, 3, 0):
        for dz in range(2):
            block(dx, 2, dz)
    for u in range(UNITS):
        first_a(1, u)
    for dx in (1, 3, 0):
        for dy in (1, 3, 0):
            for dz in range(2):
                block(dx, dy, dz)
    for o, u in units:
        direct_a(o, u)

    for copy in tot_x:
        copy.wait_recv()
    tot[1] = tot[0] + tot_recv[0] + tot_recv[1] + tot_recv[2]
    tot_y = [send("t", tot.at[1], tot_recv.at[d + 2], at_y(d)) for d in (1, 2, 3)]

    for o, u in units:
        second_a(o, u)
    for copy in tot_y:
        copy.wait_recv()
    tot[2] = tot[1] + tot_recv[3] + tot_recv[4] + tot_recv[5]
    tot_z = send("t", tot.at[2], tot_recv.at[6], at_z)

    for o, u in units:
        last_a(o, u)
        first_b(o, u)
    for o, u in units:
        second_b(o, u)
    tot_z.wait_recv()
    whole = tot[2] + tot_recv[6]
    divisors = []
    blank = jnp.zeros((32, 64), F32)
    for k in range(2):
        table_k = jnp.concatenate([whole[:, k * 64:(k + 1) * 64], blank], axis=1)
        columns = []
        for b in range(BLOCK // 128):
            index = jnp.concatenate([shells(mine * BLOCK, b)] * 4, axis=0)
            columns.append(lanes(table_k, index) + 1.0)
        divisors.append(columns)
    for o, u in units:
        last_b(o, u)
    for o, u in units:
        z_c[o, u].wait_recv()
        for h in range(2):
            done = part_c[o, u, 0, h] + z_recv[o, u, h]
            for b in range(2):
                low = (o * UNITS + u) * ROWS
                below = divisors[o][2 * h + b][u * ROWS:(u + 1) * ROWS]
                out_ref[low:low + ROWS, pl.ds(h * HALF + b * 128, 128)] = done[:, b * 128:(b + 1) * 128] / below

    for copy in sent:
        copy.wait_send()


def shards(images, references, orientations, ctf_table, inv_noise, class_weight):
    classes, planes, width = references.shape
    vmem = pl.BlockSpec(memory_space=pltpu.VMEM)
    hbm = pl.BlockSpec(memory_space=pl.ANY)
    dma = pltpu.SemaphoreType.DMA
    blocks = WIDTH // (2 * BLOCK)
    out = pl.pallas_call(
        kernel,
        out_shape=jax.ShapeDtypeStruct((KP, BLOCK), F32),
        in_specs=[hbm, hbm, vmem, vmem, vmem, pl.BlockSpec(memory_space=pltpu.SMEM)],
        out_specs=vmem,
        scratch_shapes=[
            pltpu.VMEM((STEPS, IMG, CHUNK), BF16),
            pltpu.VMEM((STEPS, KP, CHUNK), BF16),
            pltpu.VMEM((blocks, 2 * IMG, BLOCK), BF16),
            pltpu.VMEM((blocks, IMG, BLOCK), F32),
            pltpu.VMEM((blocks, IMG, BLOCK), F32),
            pltpu.VMEM((IMG, SHELLS), F32),
            pltpu.VMEM((KP + 8, 128), F32),
            pltpu.VMEM((3, 8, 128), F32),
            pltpu.VMEM((3, 8, 128), F32),
            pltpu.VMEM((KP + 8, 128), F32),
            pltpu.VMEM((2, UNITS, 2, 4, 4, 2, ROWS, HALF), F32),
            pltpu.VMEM((2, UNITS, 2, 4, 2, ROWS, HALF), F32),
            pltpu.VMEM((2, UNITS, 2, 2, ROWS, HALF), F32),
            pltpu.VMEM((2, UNITS, 2, 4, 2, ROWS, HALF), F32),
            pltpu.VMEM((2, UNITS, 2, 4, 2, ROWS, HALF), F32),
            pltpu.VMEM((2, UNITS, 2, 4, 2, ROWS, HALF), F32),
            pltpu.VMEM((2, UNITS, 2, 2, ROWS, HALF), F32),
            pltpu.VMEM((2, UNITS, 2, 2, ROWS, HALF), F32),
            pltpu.VMEM((2, UNITS, 2, 2, ROWS, HALF), F32),
            pltpu.VMEM((2, UNITS, 2, ROWS, HALF), F32),
            pltpu.VMEM((3, 32, 128), F32),
            pltpu.VMEM((7, 32, 128), F32),
            pltpu.VMEM((KP, IMG), F32),
            dma((STEPS,)), dma((STEPS,)), dma((STEPS,)), dma((STEPS,)),
            dma((8,)), dma((8,)),
            dma((12 * UNITS,)), dma((12 * UNITS,)),
            dma((14 * UNITS,)), dma((14 * UNITS,)),
            dma((7,)), dma((7,)),
        ],
        compiler_params=pltpu.CompilerParams(
            collective_id=0, has_side_effects=True, vmem_limit_bytes=60 * 2**20
        ),
        name="em_step",
    )(
        images,
        references.reshape(classes * planes, width),
        orientations,
        ctf_table,
        inv_noise.reshape(1, IMG),
        class_weight,
    )
    return out.reshape(classes, planes, BLOCK)


def solution(mesh):
    return jax.shard_map(
        shards,
        mesh=mesh,
        in_specs=(
            P("img", None),
            P(None, "slab", None),
            P("img", None, None),
            P("img", None),
            P("img"),
            P(),
        ),
        out_specs=P(None, "slab", "img"),
        check_vma=False,
    )
```

time: 658 us -> 58.3 us (0.09); the launches traced: 651 us -> 58.1 us
  waiting for transfers between devices: 310 us -> 0 us
  local copies, waits for them, and re-layouts: 184 us -> 1.57 us
  other arithmetic: 89.7 us -> 0 us
  Pallas kernels: 0 us -> 56.6 us
  matrix products: 36.2 us -> 0 us
  blocking collectives: 17.4 us -> 0 us
  between operations: 13.5 us -> 0.01 us
    reduce_scatter x1 -> x0, waiting for transfers between devices: 310 us -> none  [shards(): lax.psum_scatter(jnp.concatenate([contract_first(weighted, flat_plane), c...]
    gather x3 -> x0, local copies, waits for them, and re-layouts: 75.1 us -> none  [shards(): picked = jnp.take_along_axis(table, orientations, axis=2)]
    reduce_sum x3 -> x0, other arithmetic: 74.7 us -> none  [the longest x1 73.2 us: shards(): power = jnp.sum(spread * spread, axis=2).astype(jnp.bfloat16)]
    mul x2 -> x0, local copies, waits for them, and re-layouts: 74.5 us -> none  [shards(): power = jnp.sum(spread * spread, axis=2).astype(jnp.bfloat16)]
    pallas_call x0 -> x1, Pallas kernels: none -> 56.6 us  [shards(): pl.pallas_call(kernel, out_shape=jax.ShapeDtypeStruct((KP, BLOCK), F32),...]
    dot_general x6 -> x0, matrix products: 36.2 us -> none  [the longest x2 17.7 us: contract_first(): lax.dot_general(left, right, (((0,), (0,)), ((), ())), preferred_element_...]
    all_gather x1 -> x0, blocking collectives: 17.4 us -> none  [shards(): table = lax.all_gather(local_table, 'slab', axis=2, tiled=True)]
    broadcast_in_dim x2 -> x0, local copies, waits for them, and re-layouts: 15.2 us -> none  [the longest x1 9.59 us: shards(): jnp.repeat(ctf_pixel, 2, axis=1)]
  transfers between devices with their start and end apart: 1 -> 0, of which waited for: 1 -> 0; matrix products, arithmetic and copies ran while one was open for 0% -> 0% of each run, Pallas kernels for 0% -> 0%
where the time goes in v1:
time: 58.3 us; the launch traced here: 58.1 us
  Pallas kernels  56.6 us (97%)
  local copies, waits for them, and re-layouts  1.57 us (3%)
    pallas_call x1, Pallas kernels, shards(): pl.pallas_call(kernel, out_shape=jax.ShapeDtypeStruct((KP, BLOCK), F32),...  56.6 us
    unnamed x1, local copies, waits for them, and re-layouts  1.57 us

profile of v1, /device:TPU:2, one launch (start us, length us, event | category | flops | bytes accessed | tf_op | source)
XLA Modules:
  0.0 58.1 jit_solution(176738861462980674)
XLA Ops:
  0.0 56.6 %em_step.1 = f32[64,512]{1,0:T(8,128)} custom-call(bf16[64,32768]{1,0:T(8,128)(2,1)} %img_hbm.1, bf16[64,32768]{1,0:T(8,128)(2,1)} %bitcast.3, s32[64,2,64]{2,1,0:T(2,128)} %orient_ref.1, f32[64,64]{1,0:T(8,128)} %ctf_ref.1, f32[1,64]{1,0:T(1,128)} %bitcast.5, f32[2]{0:T(128)} %prior_ref.1), custom_call_target="tpu_custom_call" | custom-call | tf_op jit(solution)/shard_map/em_step/pallas_call | solution.py:340
  56.6 1.6 %copy.8 = f32[2,32,512]{2,1,0:T(8,128)} copy(f32[2,32,512]{2,1,0:T(8,128)} %bitcast.4) | data formatting | bytes 262144

commit v2 on v1

v2 whole, which is shorter than its diff:
```python
import functools

import jax
import jax.numpy as jnp
from jax import lax
from jax.experimental import pallas as pl
from jax.experimental.pallas import tpu as pltpu
from jax.sharding import PartitionSpec as P

BOX = 128
SHELLS = 64
KP = 64
IMG = 64
WIDTH = 32768
BLOCK = 512
OWNERS = WIDTH // (2 * BLOCK)
PAIR = 2048
PAIRS = WIDTH // PAIR
ROWS = 8
UNITS = 3
COPIES = 144
HALF = 256
LOWEST = -3.0e38
MESH = pl.DeviceIdType.MESH
F32 = jnp.float32
BF16 = jnp.bfloat16


def lanes(table, index):
    return jnp.take_along_axis(table, index, axis=1, mode="promise_in_bounds")


def flat(core, x, z, y):
    return ((y * 2 + z) * 4 + x) * 2 + core


def kernel(
    img_hbm, ref_hbm, orient_ref, ctf_ref, noise_ref, prior_ref, out_ref,
    img_v, ref_v, near_w, w_send, w_recv, ctf_a, square_a, ctf_b, square_b, ctf_send, ctf_other,
    stat_send, stat_own, stat_other, pair_recv,
    part_a, fwd_a, dir_a, sum_a, part_b, fwd_b, dir_b, sum_b, part_c, z_recv,
    part_q, q_z, q_fwd, q_dir, q_sum, q_b, q_recv,
    tot, tot_recv, counts,
    img_sem, ref_sem, w_ssem, w_rsem, ssem, rsem,
):
    mine = lax.axis_index("img")
    slab = lax.axis_index("slab")
    core, x = mine % 2, (mine // 2) % 4
    z, y = (mine // 8) % 2, mine // 16

    def at_x(d):
        return (flat(core, (x + d) % 4, z, y), slab)

    def at_y(d):
        return (flat(core, x, z, (y + d) % 4), slab)

    at = (at_x, at_y)
    at_z = (flat(core, x, 1 - z, y), slab)
    sibling = (flat(1 - core, x, z, y), slab)

    peers = [sibling, at_z]
    peers += [at_x(d) for d in (1, 2, 3)] + [at_y(d) for d in (1, 2, 3)]
    for d in (1, 2, 3):
        peers.append((mine, (slab + d) % 4))
        peers.append((flat(1 - core, x, z, y), (slab + d) % 4))
    barrier = pltpu.get_barrier_semaphore()
    for peer in peers:
        pl.semaphore_signal(barrier, inc=1, device_id=peer, device_id_type=MESH)

    def load(pair):
        span = pl.ds(pl.multiple_of(pair * PAIR, PAIR), PAIR)
        return (
            pltpu.make_async_copy(img_hbm.at[:, span], img_v.at[pair], img_sem.at[pair]),
            pltpu.make_async_copy(ref_hbm.at[:, span], ref_v.at[pair], ref_sem.at[pair]),
        )

    for g in range(PAIRS // 2):
        for pair in (PAIRS // 2 + g, PAIRS // 2 - 1 - g):
            for copy in load(pair):
                copy.start()

    own = jnp.concatenate([orient_ref[:, 0, :], orient_ref[:, 1, :]], axis=1).astype(F32)
    own = jnp.transpose(own) - (slab * 32).astype(F32)
    for k in range(2):
        listed = own[k * 64:(k + 1) * 64]
        for p in range(32):
            hit = jnp.where(listed == float(p), 1.0, 0.0)
            counts[k * 32 + p:k * 32 + p + 1, :] = jnp.sum(hit, axis=0, keepdims=True)

    table = jnp.concatenate([ctf_ref[...], jnp.zeros((IMG, 64), F32)], axis=1)
    ctf_send[...] = table
    lane = lax.broadcasted_iota(jnp.int32, (8, 128), 1)
    near = (lane // 2 - 64).astype(F32)
    far = (lane // 2).astype(F32)
    squares = (0.5 * near * near + 0.25, 0.5 * far * far + 0.25)

    def shells(row, b):
        radius = squares[b % 2] + 0.5 * (row * row).astype(F32)
        return jnp.minimum(jnp.sqrt(radius), 63.0).astype(jnp.int32)

    def spread(slot, first, start):
        ctf_rows, square_rows = slot
        for k in range(start, 9):
            for b in range(2):
                cut = slice(b * 128, (b + 1) * 128)
                index = jnp.concatenate([shells(first + k, b)] * 8, axis=0)
                ctf = lanes(table, index)
                ctf_rows[k, :, cut] = ctf
                square_rows[k, :, cut] = (ctf * ctf * -0.5).astype(BF16)

    def follow(slot, last, first):
        slot[0][0] = last[0][8]
        slot[1][0] = last[1][8]
        spread(slot, first, 1)

    def last_dims(left, right):
        return lax.dot_general(left, right, (((1,), (1,)), ((), ())), preferred_element_type=F32)

    def score(g, slot, fit):
        ctf_rows, square_rows = slot
        high, low = PAIRS // 2 + g, PAIRS // 2 - 1 - g
        for m in range(0, 9, 3):
            powers, squares_here = [], []
            for k in range(m, m + 3):
                power = None
                if k < 8:
                    entries = ref_v[high, :, k * 256:(k + 1) * 256].astype(F32)
                    power = entries * entries
                if k > 0:
                    entries = ref_v[low, :, (8 - k) * 256:(9 - k) * 256].astype(F32)
                    power = entries * entries if power is None else power + entries * entries
                powers.append(power.astype(BF16))
                squares_here.append(square_rows[k])
            fit = fit + last_dims(jnp.concatenate(powers, axis=1), jnp.concatenate(squares_here, axis=1))
        for pair, mirrored in ((high, False), (low, True)):
            for n in range(2):
                t = pair * 2 + n
                for other in (True, False):
                    part = 1 - core if other else core
                    inner = pl.multiple_of(n * 2 * BLOCK + part * BLOCK, BLOCK)
                    pixels = img_v[pair, :, pl.ds(inner, BLOCK)]
                    entries = ref_v[pair, :, pl.ds(inner, BLOCK)]
                    ws = []
                    for e in range(2):
                        k = 4 * n + 2 * part + e
                        k = 8 - k if mirrored else k
                        ws.append((pixels[:, e * 256:(e + 1) * 256].astype(F32) * ctf_rows[k]).astype(BF16))
                    w = jnp.concatenate(ws, axis=1)
                    fit = fit + last_dims(entries, w)
                    if other:
                        w_send[t] = w.astype(F32)
                    else:
                        near_w[t] = w
        return fit

    def twice(i, fit):
        for g in (2 * i, 2 * i + 1):
            for pair in (PAIRS // 2 + g, PAIRS // 2 - 1 - g):
                for copy in load(pair):
                    copy.wait()
        follow(slot_b, slot_a, i * 16 + 8)
        fit = score(2 * i, slot_a, fit)
        follow(slot_a, slot_b, i * 16 + 16)
        return score(2 * i + 1, slot_b, fit)

    slot_a, slot_b = (ctf_a, square_a), (ctf_b, square_b)
    spread(slot_a, jnp.int32(0), 0)
    fit = lax.fori_loop(0, PAIRS // 4, twice, jnp.zeros((KP, IMG), F32))

    upper = lax.broadcasted_iota(jnp.int32, (KP, IMG), 0) < 32
    prior = jnp.log(jnp.where(upper, prior_ref[0], prior_ref[1]))
    value = prior + noise_ref[...] * (2.0 * fit)
    count = counts[...]
    listed = count > 0.0
    peak = jnp.max(jnp.where(listed, value, LOWEST), axis=0, keepdims=True)
    weight = jnp.where(listed, count * jnp.exp(value - peak), 0.0)
    mass = jnp.sum(weight, axis=0, keepdims=True)
    stat_send[0:KP, 0:IMG] = weight
    stat_send[KP:KP + 1, 0:IMG] = peak
    stat_send[KP + 1:KP + 2, 0:IMG] = mass

    pl.semaphore_wait(barrier, len(peers))

    sent = []

    def send(src, dst, peer):
        n = len(sent)
        copy = pltpu.make_async_remote_copy(
            src_ref=src, dst_ref=dst, send_sem=ssem.at[n], recv_sem=rsem.at[n],
            device_id=peer, device_id_type=MESH,
        )
        copy.start()
        sent.append(copy)
        return copy

    stats = stat_send.at[pl.ds(KP, 8), :]
    waits = []
    for d in (2, 1, 3):
        waits.append(send(stats, stat_own.at[d - 1], (mine, (slab + d) % 4)))
        waits.append(send(stats, stat_other.at[d - 1], (flat(1 - core, x, z, y), (slab + d) % 4)))
    waits.append(send(stat_send, pair_recv, sibling))
    ctf_copy = send(ctf_send, ctf_other, sibling)

    order = [(2, dy, dz) for dy in (2, 1, 3, 0) for dz in (1, 0)]
    order += [(dx, 2, dz) for dx in (1, 3, 0) for dz in (1, 0)]
    order += [(dx, dy, 1) for dx in (1, 3, 0) for dy in (1, 3, 0)]
    order += [(dx, dy, 0) for dx in (1, 3, 0) for dy in (1, 3, 0)]

    def owner(dx, dy, dz):
        return (((y + dy) % 4) * 2 + (z + dz) % 2) * 4 + (x + dx) % 4

    w_copies = {}
    for n, place in enumerate(order):
        w_copies[place] = pltpu.make_async_remote_copy(
            src_ref=w_send.at[owner(*place)], dst_ref=w_recv.at[n], send_sem=w_ssem.at[n],
            recv_sem=w_rsem.at[n], device_id=sibling, device_id_type=MESH,
        )
        w_copies[place].start()

    for copy in waits:
        copy.wait_recv()

    def share(first, second, rest):
        top = first
        for d in range(3):
            top = jnp.maximum(top, rest[d, 0:1, 0:IMG])
        total = second * jnp.exp(first - top)
        for d in range(3):
            total = total + rest[d, 1:2, 0:IMG] * jnp.exp(rest[d, 0:1, 0:IMG] - top)
        return jnp.exp(first - top) / total

    here = weight * share(peak, mass, stat_own)
    there = pair_recv[0:KP, 0:IMG] * share(pair_recv[KP:KP + 1, 0:IMG], pair_recv[KP + 1:KP + 2, 0:IMG], stat_other)
    planes = jnp.concatenate([here, there], axis=1).astype(BF16)

    def block(n):
        dx, dy, dz = order[n]
        both = jnp.concatenate([near_w[owner(dx, dy, dz)], w_recv[n].astype(BF16)], axis=0)
        got = jnp.dot(planes, both, preferred_element_type=F32)
        for h in range(2):
            cut = slice(h * HALF, (h + 1) * HALF)
            for o in range(2):
                first, second = (dx, dy) if o == 0 else (dy, dx)
                for u in range(UNITS + 1):
                    row = (o * (UNITS + 1) + u) * ROWS
                    piece = got[row:row + ROWS, cut]
                    if u < UNITS:
                        part_a[o, u, h, first, second, dz] = piece
                    else:
                        part_q[o, dz, h, first, second] = piece

    def blocks(start, stop):
        for n in range(start, stop):
            w_copies[order[n]].wait_recv()
        for n in range(start, stop):
            block(n)

    f_a, g_a, h_a, f_b, g_b, h_b, z_c = {}, {}, {}, {}, {}, {}, {}
    z_q, f_q, g_q, h_q, d_q = {}, {}, {}, {}, {}

    def ahead(part, into, to):
        return [send(part.at[0, 2], into.at[0], to(1)), send(part.at[1, 2], into.at[1], to(3))]

    def direct(part, into, to):
        return [send(part.at[0, 3], into.at[0], to(3)), send(part.at[1, 1], into.at[1], to(1))]

    def onward(part, came, copies, into, to):
        out = []
        for h, d in ((0, 1), (1, 3)):
            copies[h].wait_recv()
            part[h, d] = part[h, d] + came[h]
            out.append(send(part.at[h, d], into.at[h], to(d)))
        return out

    def first_a(o, u):
        f_a[o, u] = ahead(part_a.at[o, u], fwd_a.at[o, u], at[o])

    def direct_a(o, u):
        g_a[o, u] = direct(part_a.at[o, u], dir_a.at[o, u], at[o])

    def second_a(o, u):
        h_a[o, u] = onward(part_a.at[o, u], fwd_a.at[o, u], f_a[o, u], sum_a.at[o, u], at[o])

    def last_a(o, u):
        for h in range(2):
            g_a[o, u][h].wait_recv()
            h_a[o, u][h].wait_recv()
            part_b[o, u, h] = part_a[o, u, h, 0] + dir_a[o, u, h] + sum_a[o, u, h]
        f_b[o, u] = ahead(part_b.at[o, u], fwd_b.at[o, u], at[1 - o])
        g_b[o, u] = direct(part_b.at[o, u], dir_b.at[o, u], at[1 - o])

    def second_b(o, u):
        h_b[o, u] = onward(part_b.at[o, u], fwd_b.at[o, u], f_b[o, u], sum_b.at[o, u], at[1 - o])

    def last_b(o, u):
        for h in range(2):
            g_b[o, u][h].wait_recv()
            h_b[o, u][h].wait_recv()
            done = part_b[o, u, h, 0] + dir_b[o, u, h] + sum_b[o, u, h]
            for dz in range(2):
                part_c[o, u, dz, h] = done[dz]
        z_c[o, u] = send(part_c.at[o, u, 1], z_recv.at[o, u], at_z)

    def first_q(o):
        z_q[o].wait_recv()
        part_q[o, 0] = part_q[o, 0] + q_z[o]
        f_q[o] = ahead(part_q.at[o, 0], q_fwd.at[o], at[o])
        g_q[o] = direct(part_q.at[o, 0], q_dir.at[o], at[o])

    def second_q(o):
        h_q[o] = onward(part_q.at[o, 0], q_fwd.at[o], f_q[o], q_sum.at[o], at[o])

    def last_q(o):
        for h in range(2):
            g_q[o][h].wait_recv()
            h_q[o][h].wait_recv()
            done = part_q[o, 0, h, 0] + q_dir[o, h] + q_sum[o, h]
            for d in range(4):
                q_b[o, d, h] = done[d]
        d_q[o] = [send(q_b.at[o, d], q_recv.at[o, d - 1], at[1 - o](d)) for d in (2, 1, 3)]

    blocks(0, 8)
    for u in range(UNITS):
        first_a(0, u)
    blocks(8, 14)
    for u in range(UNITS):
        first_a(1, u)
    blocks(14, 23)
    for o in range(2):
        z_q[o] = send(part_q.at[o, 1], q_z.at[o], at_z)
    blocks(23, 32)
    for o in range(2):
        direct_a(o, 0)

    ctf_copy.wait_recv()
    squared = jnp.concatenate([ctf_ref[...], ctf_other[:, 0:SHELLS]], axis=0)
    squared = (squared * squared).astype(BF16)
    shell_sum = jnp.dot(planes, squared, preferred_element_type=F32)
    tot[0] = jnp.concatenate([shell_sum[0:32], shell_sum[32:64]], axis=1)
    tot_x = [send(tot.at[0], tot_recv.at[d - 1], at_x(d)) for d in (1, 2, 3)]

    both = (0, 1)
    for u in range(UNITS):
        for o in both:
            second_a(o, u)
        if u + 1 < UNITS:
            for o in both:
                direct_a(o, u + 1)
    for copy in w_copies.values():
        copy.wait_send()
    for copy in tot_x:
        copy.wait_recv()
    tot[1] = tot[0] + tot_recv[0] + tot_recv[1] + tot_recv[2]
    tot_y = [send(tot.at[1], tot_recv.at[d + 2], at_y(d)) for d in (1, 2, 3)]
    first_q(0)
    for o in both:
        last_a(o, 0)
    for o in both:
        last_a(o, 1)
    for copy in tot_y:
        copy.wait_recv()
    tot[2] = tot[1] + tot_recv[3] + tot_recv[4] + tot_recv[5]
    tot_z = send(tot.at[2], tot_recv.at[6], at_z)
    first_q(1)
    for o in both:
        last_a(o, 2)
    for o in both:
        second_b(o, 0)
    second_q(0)
    for o in both:
        second_b(o, 1)
    second_q(1)
    for o in both:
        second_b(o, 2)
    for o in both:
        last_b(o, 0)
    last_q(0)
    for o in both:
        last_b(o, 1)
    last_q(1)
    for o in both:
        last_b(o, 2)
    early = len(sent) - 40
    for copy in sent[:early]:
        copy.wait_send()

    tot_z.wait_recv()
    whole = tot[2] + tot_recv[6]
    divisors = []
    blank = jnp.zeros((32, 64), F32)
    for k in range(2):
        table_k = jnp.concatenate([whole[:, k * 64:(k + 1) * 64], blank], axis=1)
        columns = []
        for b in range(BLOCK // 128):
            row = mine * 2 + b // 2 - 64
            index = jnp.concatenate([shells(row, b)] * 4, axis=0)
            columns.append(lanes(table_k, index) + 1.0)
        divisors.append(columns)

    def finish(o, u, h, done):
        low = (o * (UNITS + 1) + u) * ROWS
        for b in range(2):
            below = divisors[o][2 * h + b][u * ROWS:(u + 1) * ROWS]
            out_ref[low:low + ROWS, pl.ds(h * HALF + b * 128, 128)] = done[:, b * 128:(b + 1) * 128] / below

    for u in range(UNITS):
        for o in range(2):
            z_c[o, u].wait_recv()
            for h in range(2):
                finish(o, u, h, part_c[o, u, 0, h] + z_recv[o, u, h])
    for o in range(2):
        for copy in d_q[o]:
            copy.wait_recv()
        for h in range(2):
            finish(o, UNITS, h, q_b[o, 0, h] + q_recv[o, 0, h] + q_recv[o, 1, h] + q_recv[o, 2, h])

    for copy in sent[early:]:
        copy.wait_send()


def shards(images, references, orientations, ctf_table, inv_noise, class_weight):
    classes, planes, width = references.shape
    vmem = pl.BlockSpec(memory_space=pltpu.VMEM)
    hbm = pl.BlockSpec(memory_space=pl.ANY)
    dma = pltpu.SemaphoreType.DMA
    out = pl.pallas_call(
        kernel,
        out_shape=jax.ShapeDtypeStruct((KP, BLOCK), F32),
        in_specs=[hbm, hbm, vmem, vmem, vmem, pl.BlockSpec(memory_space=pltpu.SMEM)],
        out_specs=vmem,
        scratch_shapes=[
            pltpu.VMEM((PAIRS, IMG, PAIR), BF16),
            pltpu.VMEM((PAIRS, KP, PAIR), BF16),
            pltpu.VMEM((OWNERS, IMG, BLOCK), BF16),
            pltpu.VMEM((OWNERS, IMG, BLOCK), F32),
            pltpu.VMEM((OWNERS, IMG, BLOCK), F32),
            pltpu.VMEM((9, IMG, 256), F32),
            pltpu.VMEM((9, IMG, 256), BF16),
            pltpu.VMEM((9, IMG, 256), F32),
            pltpu.VMEM((9, IMG, 256), BF16),
            pltpu.VMEM((IMG, 128), F32),
            pltpu.VMEM((IMG, 128), F32),
            pltpu.VMEM((KP + 8, 128), F32),
            pltpu.VMEM((3, 8, 128), F32),
            pltpu.VMEM((3, 8, 128), F32),
            pltpu.VMEM((KP + 8, 128), F32),
            pltpu.VMEM((2, UNITS, 2, 4, 4, 2, ROWS, HALF), F32),
            pltpu.VMEM((2, UNITS, 2, 4, 2, ROWS, HALF), F32),
            pltpu.VMEM((2, UNITS, 2, 4, 2, ROWS, HALF), F32),
            pltpu.VMEM((2, UNITS, 2, 4, 2, ROWS, HALF), F32),
            pltpu.VMEM((2, UNITS, 2, 4, 2, ROWS, HALF), F32),
            pltpu.VMEM((2, UNITS, 2, 2, ROWS, HALF), F32),
            pltpu.VMEM((2, UNITS, 2, 2, ROWS, HALF), F32),
            pltpu.VMEM((2, UNITS, 2, 2, ROWS, HALF), F32),
            pltpu.VMEM((2, UNITS, 2, 2, ROWS, HALF), F32),
            pltpu.VMEM((2, UNITS, 2, ROWS, HALF), F32),
            pltpu.VMEM((2, 2, 2, 4, 4, ROWS, HALF), F32),
            pltpu.VMEM((2, 2, 4, 4, ROWS, HALF), F32),
            pltpu.VMEM((2, 2, 4, ROWS, HALF), F32),
            pltpu.VMEM((2, 2, 4, ROWS, HALF), F32),
            pltpu.VMEM((2, 2, 4, ROWS, HALF), F32),
            pltpu.VMEM((2, 4, 2, ROWS, HALF), F32),
            pltpu.VMEM((2, 3, 2, ROWS, HALF), F32),
            pltpu.VMEM((3, 32, 128), F32),
            pltpu.VMEM((7, 32, 128), F32),
            pltpu.VMEM((KP, IMG), F32),
            dma((PAIRS,)), dma((PAIRS,)), dma((OWNERS,)), dma((OWNERS,)), dma((COPIES,)), dma((COPIES,)),
        ],
        compiler_params=pltpu.CompilerParams(
            collective_id=0, has_side_effects=True, vmem_limit_bytes=60 * 2**20
        ),
        name="em_step",
    )(
        images,
        references.reshape(classes * planes, width),
        orientations,
        ctf_table,
        inv_noise.reshape(1, IMG),
        class_weight,
    )
    return out.reshape(classes, planes, BLOCK)


def solution(mesh):
    return jax.shard_map(
        shards,
        mesh=mesh,
        in_specs=(
            P("img", None),
            P(None, "slab", None),
            P("img", None, None),
            P("img", None),
            P("img"),
            P(),
        ),
        out_specs=P(None, "slab", "img"),
        check_vma=False,
    )
```

time: 58.3 us -> 50.3 us (0.86); the launches traced: 58.1 us -> 49.3 us
  Pallas kernels: 56.6 us -> 47.8 us
    pallas_call x1, Pallas kernels: 56.6 us -> 47.8 us  [shards(): pl.pallas_call(kernel, out_shape=jax.ShapeDtypeStruct((KP, BLOCK), F32),...]
where the time goes in v2:
time: 50.3 us; the launch traced here: 49.3 us
  Pallas kernels  47.8 us (95%)
  local copies, waits for them, and re-layouts  1.57 us (3%)
    pallas_call x1, Pallas kernels, shards(): pl.pallas_call(kernel, out_shape=jax.ShapeDtypeStruct((KP, BLOCK), F32),...  47.8 us
    unnamed x1, local copies, waits for them, and re-layouts  1.57 us

profile of v2, /device:TPU:2, one launch (start us, length us, event | category | flops | bytes accessed | tf_op | source)
XLA Modules:
  0.0 49.3 jit_solution(15989560043133712951)
XLA Ops:
  0.0 47.8 %em_step.1 = f32[64,512]{1,0:T(8,128)} custom-call(bf16[64,32768]{1,0:T(8,128)(2,1)} %img_hbm.1, bf16[64,32768]{1,0:T(8,128)(2,1)} %bitcast.3, s32[64,2,64]{2,1,0:T(2,128)} %orient_ref.1, f32[64,64]{1,0:T(8,128)} %ctf_ref.1, f32[1,64]{1,0:T(1,128)} %bitcast.5, f32[2]{0:T(128)} %prior_ref.1), custom_call_target="tpu_custom_call" | custom-call | tf_op jit(solution)/shard_map/em_step/pallas_call | solution.py:426
  47.8 1.6 %copy.8 = f32[2,32,512]{2,1,0:T(8,128)} copy(f32[2,32,512]{2,1,0:T(8,128)} %bitcast.4) | data formatting | bytes 262144
